TPU v7x, 256 devices: a whole 4x4x8 slice. The times are simulated.
256 devices in a mesh: ctx: 128 (over y, x, z), head: 2 (over core).
Axes of the slice: x: 4, y: 4, z: 8, core: 2. Of those that a mesh axis runs over, the one named last changes fastest.
Arguments:
- queries: bfloat16 [16384, 64, 128], P('ctx', 'head'), may hold values from -90 to 90
- key_heads: bfloat16 [16384, 8, 128], P('ctx', 'head'), may hold values from -4 to 4
- value_head_rows: bfloat16 [16384, 8, 128], P('ctx', 'head'), may hold values from -6 to 6
- doc_lengths: int32 [64], replicated, may hold values from 1 to 512, 16384 in all
Outputs:
- attended: bfloat16 [16384, 64, 128], P(('ctx', 'head'))
Inputs may be any that keep to these rules, and one draw needn't show every extreme that they name: `doc_lengths`: lengths of 64 documents in order, summing to 16384; the longest is exactly 512.
All inputs are finite; a program needn't handle non-finite values.
Results may differ from a plain program's by a relative error of at most 0.0055.
Values may be sent and summed in bfloat16 or wider, within the bound.
A program may use at most 128 MiB of HBM per device.

v0:
```python
import functools
import math

import jax
import jax.numpy as jnp
from jax import lax
from jax.experimental import pallas as pl
from jax.experimental.pallas import tpu as pltpu
from jax.sharding import PartitionSpec as P

REACH = 8
MASKED = -1e30
MESH = pl.DeviceIdType.MESH


def kernel(
    ctx_count,
    q_hbm,
    k_hbm,
    v_hbm,
    len_hbm,
    o_hbm,
    q_scr,
    kv,
    kv_out,
    raw,
    wide,
    bias,
    acc,
    total,
    largest,
    o_scr,
    lens,
    raw_sem,
    len_sem,
    q_sem,
    q_send_sem,
    o_sem,
    recv_sem,
    send_sem,
    pair_sem,
):
    kv_heads = k_hbm.shape[1]
    group = q_hbm.shape[1] // kv_heads
    rows = k_hbm.shape[0] // 2
    width = k_hbm.shape[2]
    docs = len_hbm.shape[0]
    nodes = 2 * ctx_count
    scale = math.log2(math.e) / math.sqrt(width)

    chip = lax.axis_index("ctx")
    core = lax.axis_index("head")
    other = 1 - core
    node = jnp.where(core == 0, chip, nodes - 1 - chip)

    def device(n):
        n = lax.rem(n + nodes, nodes)
        return (jnp.where(n < ctx_count, n, nodes - 1 - n), jnp.where(n < ctx_count, 0, 1))

    pair = (chip, other)
    above, below = device(node + 1), device(node - 1)
    far, far_back = device(node + REACH), device(node - REACH)

    local = []
    for part, half in enumerate((core, other)):
        for which, source in enumerate((k_hbm, v_hbm)):
            copy = pltpu.make_async_copy(
                source.at[pl.ds(pl.multiple_of(half * rows, rows), rows)],
                raw.at[part, which],
                raw_sem.at[part, which],
            )
            copy.start()
            local.append(copy)
    len_copy = pltpu.make_async_copy(len_hbm, lens, len_sem)
    len_copy.start()
    q_local, q_remote = [], []
    for k in range(kv_heads):
        copy = pltpu.make_async_copy(
            q_hbm.at[pl.ds(pl.multiple_of(core * rows, rows), rows), pl.ds(k * group, group)],
            q_scr.at[core * kv_heads + k],
            q_sem.at[core, k],
        )
        copy.start()
        q_local.append(copy)
        q_remote.append(
            pltpu.make_async_remote_copy(
                src_ref=q_hbm.at[
                    pl.ds(pl.multiple_of(other * rows, rows), rows), pl.ds(k * group, group)
                ],
                dst_ref=q_scr.at[core * kv_heads + k],
                send_sem=q_send_sem.at[k],
                recv_sem=q_sem.at[core, k],
                device_id=pair,
                device_id_type=MESH,
            )
        )

    barrier = pltpu.get_barrier_semaphore()
    for target in (pair, above, below, far_back):
        pl.semaphore_signal(barrier, inc=1, device_id=target, device_id_type=MESH)

    for part in (1, 0):
        for which in range(2):
            local[2 * part + which].wait()
            wide[...] = raw[part, which].astype(jnp.float32)
            for k in range(kv_heads):
                piece = wide.reshape(rows * kv_heads, width)[
                    pl.ds(k, rows, stride=kv_heads), :
                ].astype(jnp.bfloat16)
                if part == 0:
                    kv[0, core, k, which] = piece
                else:
                    kv_out[k, which] = piece

    pl.semaphore_wait(barrier, 4)

    def to_pair():
        return pltpu.make_async_remote_copy(
            src_ref=kv_out,
            dst_ref=kv.at[0, core],
            send_sem=pair_sem,
            recv_sem=recv_sem.at[0, core],
            device_id=pair,
            device_id_type=MESH,
        )

    def send(slot, into, half, target):
        return pltpu.make_async_remote_copy(
            src_ref=kv.at[slot, half],
            dst_ref=kv.at[into, half],
            send_sem=send_sem.at[into, half],
            recv_sem=recv_sem.at[into, half],
            device_id=target,
            device_id_type=MESH,
        )

    def incoming(slot, half):
        return send(slot, slot, half, above)

    to_pair().start()
    send(0, 1, core, above).start()
    send(0, REACH, core, far).start()
    for copy in q_remote:
        copy.start()

    len_copy.wait()
    lane = lax.broadcasted_iota(jnp.int32, (8, 128), 1)

    def add_doc(j, ends):
        return ends + jnp.where(lane >= j, lens[j], 0)

    ends = lax.fori_loop(0, docs, add_doc, jnp.zeros((8, 128), jnp.int32))
    ends = jnp.where(lane < docs, ends, 0)
    ends = jnp.concatenate([ends] * rows, axis=0)
    row = lax.broadcasted_iota(jnp.int32, (rows * group, 128), 0) // group
    column = lax.broadcasted_iota(jnp.int32, (rows * group, 128), 1)
    place = node * rows + row
    begin = jnp.max(jnp.where(ends <= place, ends, 0), axis=1, keepdims=True)

    send_second = [send(0, 1, other, above), send(0, REACH, other, far)]
    incoming(0, other).wait_recv()
    for copy in send_second:
        copy.start()

    for step in range(REACH // 2 + 1):
        near, away = (0, 0) if step == 0 else (step, REACH + 1 - step)
        back = jnp.where(column < rows, near, away)
        seen = (node - back) * rows + column % rows
        allowed = (seen >= begin) & (seen <= place)
        if step == 0:
            allowed = allowed & (column < rows)
        bias[step] = jnp.where(allowed, 0.0, MASKED)

    def attend(step, half):
        slots = (0,) if step == 0 else (step, REACH + 1 - step)
        last = step == REACH // 2
        lanes = rows * len(slots)

        def one_head(k, carry):
            head = half * kv_heads + k
            queries = q_scr.reshape(2 * kv_heads, rows * group, width)[head]
            keys = jnp.concatenate([kv[s, half, k, 0] for s in slots], axis=0)
            values = jnp.concatenate([kv[s, half, k, 1] for s in slots], axis=0)
            scores = lax.dot_general(
                queries, keys, (((1,), (1,)), ((), ())), preferred_element_type=jnp.float32
            )
            scores = scores * scale + bias[step, :, :lanes]
            highest = jnp.max(scores, axis=1, keepdims=True)
            if step == 0:
                updated = jnp.broadcast_to(highest, (rows * group, width))
                weights = jnp.exp2(scores - updated[:, :lanes])
                sums = jnp.broadcast_to(
                    jnp.sum(weights, axis=1, keepdims=True), (rows * group, width)
                ) * (1.0 / width)
            else:
                earlier = largest[head]
                updated = jnp.maximum(earlier, highest)
                shrink = jnp.exp2(earlier - updated)
                weights = jnp.exp2(scores - updated)
                sums = total[head] * shrink + weights
            out = jnp.dot(
                weights.astype(jnp.bfloat16), values, preferred_element_type=jnp.float32
            )
            if step > 0:
                out = acc[head] * shrink + out
            if last:
                result = out * (1.0 / jnp.sum(sums, axis=1, keepdims=True))
                o_scr.reshape(2 * kv_heads, rows * group, width)[head] = result.astype(
                    jnp.bfloat16
                )
                write(head).start()
            else:
                acc[head] = out
                total[head] = sums
                largest[head] = updated
            return carry

        lax.fori_loop(0, kv_heads, one_head, 0)

    def write(head):
        return pltpu.make_async_copy(
            o_scr.at[head],
            o_hbm.at[:, pl.ds(pl.multiple_of(head * group, group), group)],
            o_sem.at[head],
        )

    def wait_queries(half, copies):
        for copy in copies:
            copy.wait() if half is core else copy.wait_recv()

    def forward(step, half):
        incoming(step, half).wait_recv()
        if step < REACH // 2:
            send(step, step + 1, half, above).start()
        incoming(REACH + 1 - step, half).wait_recv()
        if step < REACH // 2:
            send(REACH + 1 - step, REACH - step, half, below).start()

    q_arriving = [
        pltpu.make_async_remote_copy(
            src_ref=q_scr.at[other * kv_heads + k],
            dst_ref=q_scr.at[other * kv_heads + k],
            send_sem=q_send_sem.at[k],
            recv_sem=q_sem.at[other, k],
            device_id=pair,
            device_id_type=MESH,
        )
        for k in range(kv_heads)
    ]
    wait_queries(core, q_local)
    attend(0, core)
    forward(1, core)
    wait_queries(other, q_arriving)
    attend(0, other)
    forward(1, other)
    for step in range(1, REACH // 2 + 1):
        attend(step, core)
        if step < REACH // 2:
            forward(step + 1, core)
        attend(step, other)
        if step < REACH // 2:
            forward(step + 1, other)

    to_pair().wait_send()
    for copy in q_remote:
        copy.wait_send()
    for into in range(1, REACH + 1):
        for half in range(2):
            send(0, into, half, above).wait_send()
    for head in range(2 * kv_heads):
        write(head).wait()


def shards(queries, key_heads, value_head_rows, doc_lengths):
    kv_heads = key_heads.shape[1]
    rows = key_heads.shape[0] // 2
    width = key_heads.shape[2]
    group = queries.shape[1] // kv_heads
    heads = 2 * kv_heads
    half_steps = REACH // 2 + 1
    any_space = pl.BlockSpec(memory_space=pl.ANY)
    state = pltpu.VMEM((heads, rows * group, width), jnp.float32)
    return pl.pallas_call(
        functools.partial(kernel, lax.axis_size("ctx")),
        name="relay_attention",
        out_shape=jax.ShapeDtypeStruct((rows, heads * group, width), jnp.bfloat16),
        in_specs=[any_space] * 4,
        out_specs=any_space,
        scratch_shapes=[
            pltpu.VMEM((heads, rows, group, width), jnp.bfloat16),
            pltpu.VMEM((REACH + 1, 2, kv_heads, 2, rows, width), jnp.bfloat16),
            pltpu.VMEM((kv_heads, 2, rows, width), jnp.bfloat16),
            pltpu.VMEM((2, 2, rows, kv_heads, width), jnp.bfloat16),
            pltpu.VMEM((rows, kv_heads, width), jnp.float32),
            pltpu.VMEM((half_steps, rows * group, 128), jnp.float32),
            state,
            state,
            state,
            pltpu.VMEM((heads, rows, group, width), jnp.bfloat16),
            pltpu.SMEM(doc_lengths.shape, jnp.int32),
            pltpu.SemaphoreType.DMA((2, 2)),
            pltpu.SemaphoreType.DMA,
            pltpu.SemaphoreType.DMA((2, kv_heads)),
            pltpu.SemaphoreType.DMA((kv_heads,)),
            pltpu.SemaphoreType.DMA((heads,)),
            pltpu.SemaphoreType.DMA((REACH + 1, 2)),
            pltpu.SemaphoreType.DMA((REACH + 1, 2)),
            pltpu.SemaphoreType.DMA,
        ],
        compiler_params=pltpu.CompilerParams(
            collective_id=0, has_side_effects=True, vmem_limit_bytes=40 << 20
        ),
    )(queries, key_heads, value_head_rows, doc_lengths)


def solution(mesh):
    in_specs = (P("ctx", "head", None), P("ctx", "head", None), P("ctx", "head", None), P())
    out_specs = P(("ctx", "head"), None, None)
    return jax.shard_map(shards, mesh=mesh, in_specs=in_specs, out_specs=out_specs, check_vma=False)
```

profile of v0, /device:TPU:24, one launch (start us, length us, event | category | flops | bytes accessed | tf_op | source)
XLA Modules:
  0.0 52.3 jit_solution(9589460171148349192)
XLA Ops:
  0.0 0.0 copy-start
  0.0 1.2 %copy-done = bf16[128,32,128]{2,1,0:T(8,128)(2,1)S(1)} copy-done((bf16[128,32,128]{2,1,0:T(8,128)(2,1)S(1)}, bf16[128,32,128]{2,1,0:T(8,128)(2,1)}, u32[]{:S(2)}) %copy-start) | copy-done | bytes 1048600
  1.2 0.0 copy-start.1
  1.2 0.9 %copy-done.1 = bf16[128,4,128]{2,1,0:T(4,128)(2,1)S(1)} copy-done((bf16[128,4,128]{2,1,0:T(4,128)(2,1)S(1)}, bf16[128,4,128]{2,1,0:T(4,128)(2,1)}, u32[]{:S(2)}) %copy-start.1) | copy-done | bytes 131096
  2.1 0.0 copy-start.2
  2.1 0.9 %copy-done.2 = bf16[128,4,128]{2,1,0:T(4,128)(2,1)S(1)} copy-done((bf16[128,4,128]{2,1,0:T(4,128)(2,1)S(1)}, bf16[128,4,128]{2,1,0:T(4,128)(2,1)}, u32[]{:S(2)}) %copy-start.2) | copy-done | bytes 131096
  3.0 0.0 copy-start.3
  3.0 0.7 %copy-done.3 = s32[64]{0:T(128)S(1)} copy-done((s32[64]{0:T(128)S(1)}, s32[64]{0:T(128)}, u32[]{:S(2)}) %copy-start.3) | copy-done | bytes 280
  3.7 47.6 %relay_attention.1 = bf16[64,64,128]{2,1,0:T(8,128)(2,1)S(1)} custom-call(bf16[128,32,128]{2,1,0:T(8,128)(2,1)S(1)} %copy-done, bf16[128,4,128]{2,1,0:T(4,128)(2,1)S(1)} %copy-done.1, bf16[128,4,128]{2,1,0:T(4,128)(2,1)S(1)} %copy-done.2, s32[64]{0:T(128)S(1)} %copy-done.3), custom_call_target="tpu_custom_call" | custom-call | tf_op jit(solution)/shard_map/relay_attention/pallas_call | solution.py:283
  51.3 1.0 %copy.6 = bf16[64,64,128]{2,1,0:T(8,128)(2,1)} copy(bf16[64,64,128]{2,1,0:T(8,128)(2,1)S(1)} %relay_attention.1) | data formatting | bytes 2097152
Async XLA Ops:
  0.0 1.2 %copy-start = (bf16[128,32,128]{2,1,0:T(8,128)(2,1)S(1)}, bf16[128,32,128]{2,1,0:T(8,128)(2,1)}, u32[]{:S(2)}) copy-start(bf16[128,32,128]{2,1,0:T(8,128)(2,1)} %q_hbm.1) | copy-start | bytes 3145732
  1.2 0.9 %copy-start.1 = (bf16[128,4,128]{2,1,0:T(4,128)(2,1)S(1)}, bf16[128,4,128]{2,1,0:T(4,128)(2,1)}, u32[]{:S(2)}) copy-start(bf16[128,4,128]{2,1,0:T(4,128)(2,1)} %k_hbm.1) | copy-start | bytes 393220
  2.1 0.9 %copy-start.2 = (bf16[128,4,128]{2,1,0:T(4,128)(2,1)S(1)}, bf16[128,4,128]{2,1,0:T(4,128)(2,1)}, u32[]{:S(2)}) copy-start(bf16[128,4,128]{2,1,0:T(4,128)(2,1)} %v_hbm.1) | copy-start | bytes 393220
  3.0 0.7 %copy-start.3 = (s32[64]{0:T(128)S(1)}, s32[64]{0:T(128)}, u32[]{:S(2)}) copy-start(s32[64]{0:T(128)} %len_hbm.1) | copy-start | bytes 772
where the time goes:
time: 52.5 us; the launch traced here: 52.3 us
  Pallas kernels  47.6 us (91%)
  local copies, waits for them, and re-layouts  4.66 us (9%)
    pallas_call x1, Pallas kernels, shards(): pl.pallas_call(functools.partial(kernel, lax.axis_size('ctx')), name='rel...  47.6 us
    unnamed x9, local copies, waits for them, and re-layouts  4.66 us

commit v1 on v0

v1 whole, which is shorter than its diff:
```python
import functools
import math

import jax
import jax.numpy as jnp
from jax import lax
from jax.experimental import pallas as pl
from jax.experimental.pallas import tpu as pltpu
from jax.sharding import PartitionSpec as P

REACH = 8
MASKED = -1e30
PIECES = 4
MESH = pl.DeviceIdType.MESH

USUAL = (1, 8, 2, 7, 3, 6, 4, 5)
AT_FOLD = (
    USUAL,
    (3, 1, 2, 4, 5, 6, 8, 7),
    (5, 1, 4, 6, 2, 3, 7, 8),
    (7, 1, 6, 8, 2, 5, 3, 4),
    USUAL,
    (1, 2, 3, 5, 6, 8, 4, 7),
    (1, 2, 6, 7, 3, 5, 8, 4),
    USUAL,
)


def kernel(
    ctx_count,
    q_hbm,
    k_hbm,
    v_hbm,
    len_hbm,
    o_hbm,
    q_scr,
    q_turned,
    kv,
    kv_out,
    raw,
    wide,
    bias,
    acc,
    total,
    largest,
    o_scr,
    lens,
    raw_sem,
    len_sem,
    q_sem,
    q_send_sem,
    o_sem,
    recv_sem,
    send_sem,
    pass_sem,
    pair_sem,
):
    kv_heads = k_hbm.shape[1]
    heads = 2 * kv_heads
    group = q_hbm.shape[1] // kv_heads
    rows = k_hbm.shape[0] // 2
    width = k_hbm.shape[2]
    docs = len_hbm.shape[0]
    tall = rows * group
    nodes = 2 * ctx_count
    own_pieces = PIECES // 2
    piece_heads = heads // PIECES
    depth = REACH // 2
    scale = math.log2(math.e) / math.sqrt(width)

    chip = lax.axis_index("ctx")
    core = lax.axis_index("head")
    other = 1 - core
    node = chip + core * (nodes - 1 - 2 * chip)
    ring, spot = lax.div(node, REACH), lax.rem(node, REACH)
    rings = ctx_count // REACH
    along = lax.rem(ring, rings)
    folds = lax.div(along + 1, rings)
    folded = 1 - lax.div(along + rings - 1, rings)

    def device(n):
        leg = lax.div(n, ctx_count)
        return (n + leg * (nodes - 1 - 2 * n), leg)

    pair = (chip, other)
    above = device(ring * REACH + lax.rem(spot + 1, REACH))
    below = device(ring * REACH + lax.rem(spot + REACH - 1, REACH))
    opposite = nodes - 1 - node
    after = device(folds * opposite + (1 - folds) * lax.rem(node + REACH, nodes))
    before = device(folded * opposite + (1 - folded) * lax.rem(node + nodes - REACH, nodes))
    spot_after = spot + folds * (REACH - 1 - 2 * spot)

    def equal(a, b):
        return 1 - lax.div((a - b) * (a - b) + 63, 64)

    order = []
    for i in range(REACH):
        change = sum(
            equal(spot, place) * (AT_FOLD[place][i] - USUAL[i])
            for place in range(REACH)
            if AT_FOLD[place][i] != USUAL[i]
        )
        order.append(USUAL[i] + folded * change)

    local = []
    for part, half in enumerate((core, other)):
        for which, source in enumerate((k_hbm, v_hbm)):
            copy = pltpu.make_async_copy(
                source.at[pl.ds(pl.multiple_of(half * rows, rows), rows)],
                raw.at[part, which],
                raw_sem.at[part, which],
            )
            copy.start()
            local.append(copy)
    len_copy = pltpu.make_async_copy(len_hbm, lens, len_sem)
    len_copy.start()
    q_local, q_remote = [], []
    for k in range(kv_heads):
        copy = pltpu.make_async_copy(
            q_hbm.at[pl.ds(pl.multiple_of(core * rows, rows), rows), pl.ds(k * group, group)],
            q_scr.at[core * kv_heads + k],
            q_sem.at[core, k],
        )
        copy.start()
        q_local.append(copy)
        q_remote.append(
            pltpu.make_async_remote_copy(
                src_ref=q_hbm.at[
                    pl.ds(pl.multiple_of(other * rows, rows), rows), pl.ds(k * group, group)
                ],
                dst_ref=q_scr.at[core * kv_heads + k],
                send_sem=q_send_sem.at[k],
                recv_sem=q_sem.at[core, k],
                device_id=pair,
                device_id_type=MESH,
            )
        )

    barrier = pltpu.get_barrier_semaphore()
    for target in (pair, above, below, before):
        pl.semaphore_signal(barrier, inc=1, device_id=target, device_id_type=MESH)

    for part in (1, 0):
        for which in range(2):
            local[2 * part + which].wait()
            wide[...] = raw[part, which].astype(jnp.float32)
            for k in range(kv_heads):
                block = wide.reshape(rows * kv_heads, width)[
                    pl.ds(k, rows, stride=kv_heads), :
                ].astype(jnp.bfloat16)
                piece, head = k // piece_heads, k % piece_heads
                if part == 0:
                    kv[0, core * own_pieces + piece, head, which] = block
                else:
                    kv_out[piece, head, which] = block

    pl.semaphore_wait(barrier, 4)

    def to_pair(i):
        return pltpu.make_async_remote_copy(
            src_ref=kv_out.at[i],
            dst_ref=kv.at[0, core * own_pieces + i],
            send_sem=pair_sem.at[i],
            recv_sem=recv_sem.at[0, core * own_pieces + i],
            device_id=pair,
            device_id_type=MESH,
        )

    def send(slot, into, piece, target):
        return pltpu.make_async_remote_copy(
            src_ref=kv.at[slot, piece],
            dst_ref=kv.at[into, piece],
            send_sem=send_sem.at[into, piece],
            recv_sem=recv_sem.at[into, piece],
            device_id=target,
            device_id_type=MESH,
        )

    def incoming(slot, piece):
        return pltpu.make_async_remote_copy(
            src_ref=kv.at[slot, piece],
            dst_ref=kv.at[slot, piece],
            send_sem=pair_sem.at[0],
            recv_sem=recv_sem.at[slot, piece],
            device_id=above,
            device_id_type=MESH,
        )

    def pass_on(slot, piece):
        source = lax.rem(spot - slot + REACH, REACH)
        lacking = lax.div(source - spot_after + REACH, REACH)
        into = 2 * REACH - 1 - lacking * (source - spot_after)
        copy = pltpu.make_async_remote_copy(
            src_ref=kv.at[slot, piece],
            dst_ref=kv.at[into, piece],
            send_sem=pass_sem.at[slot, piece],
            recv_sem=recv_sem.at[into, piece],
            device_id=after,
            device_id_type=MESH,
        )
        return lacking == 1, copy

    def start_pass(slot, piece):
        lacking, copy = pass_on(slot, piece)
        pl.when(lacking)(copy.start)

    def first_sends(piece):
        send(0, 1, piece, above).start()
        send(0, REACH - 1, piece, below).start()
        start_pass(0, piece)

    def piece_at(i):
        half = lax.rem(core + lax.div(i, own_pieces), 2)
        return half * own_pieces + lax.rem(i, own_pieces)

    for i in range(own_pieces):
        to_pair(i).start()
    for i in range(own_pieces):
        first_sends(core * own_pieces + i)
    for copy in q_remote:
        copy.start()
    for i in range(own_pieces):
        incoming(0, other * own_pieces + i).wait_recv()
        first_sends(other * own_pieces + i)

    len_copy.wait()
    place = node * rows + lax.broadcasted_iota(jnp.int32, (8, tall), 1) // group

    def add_doc(j, carry):
        end, begin = carry
        end = end + lens[j]
        return end, jnp.where(place >= end, end, begin)

    _, begin = lax.fori_loop(0, docs, add_doc, (jnp.int32(0), jnp.zeros((8, tall), jnp.int32)))

    backs = [(0, 0)] + [(order[2 * i], order[2 * i + 1]) for i in range(depth)]
    key_row = lax.broadcasted_iota(jnp.int32, (8, tall), 0)
    for step, both in enumerate(backs):
        for part in range(1 if step == 0 else 2):
            base = (node - both[part]) * rows

            def fill(i, carry, step=step, part=part, base=base):
                seen = base + i * 8 + key_row
                allowed = (seen >= begin) & (seen <= place)
                at = pl.multiple_of(part * rows + i * 8, 8)
                bias[step, pl.ds(at, 8), :] = jnp.where(allowed, 0.0, MASKED)
                return carry

            lax.fori_loop(0, rows // 8, fill, 0)

    def slot_of(back):
        return back + (REACH - 1) * lax.div(back - spot + REACH - 1, REACH)

    def write(head):
        return pltpu.make_async_copy(
            o_scr.at[head],
            o_hbm.at[:, pl.ds(pl.multiple_of(head * group, group), group)],
            o_sem.at[head],
        )

    def attend(step, piece, backs, last):
        first = not backs
        for back in backs:
            pl.when(back > spot)(incoming(REACH - 1 + back, piece).wait_recv)
        slots = [slot_of(back) for back in backs] or [0]
        depth_keys = rows * len(slots)
        for i in range(piece_heads):
            head = piece * piece_heads + i
            keys = jnp.concatenate([kv[s, piece, i, 0] for s in slots], axis=0)
            values = jnp.concatenate([kv[s, piece, i, 1] for s in slots], axis=0)
            scores = jnp.dot(keys, q_turned[head], preferred_element_type=jnp.float32)
            scores = scores * scale + bias[step, :depth_keys]
            updated = jnp.max(scores, axis=0, keepdims=True)
            if not first:
                earlier = largest[head]
                updated = jnp.maximum(earlier, updated)
                shrink = jnp.exp2(earlier - updated)
            weights = jnp.exp2(scores - updated)
            sums = jnp.sum(weights, axis=0, keepdims=True)
            out = lax.dot_general(
                values,
                weights.astype(jnp.bfloat16),
                (((0,), (0,)), ((), ())),
                preferred_element_type=jnp.float32,
            )
            if not first:
                sums = total[head] * shrink + sums
                out = acc[head] * shrink + out
            if last:
                result = (out * (1.0 / sums)).T.astype(jnp.bfloat16)
                o_scr.reshape(heads, tall, width)[head] = result
                write(head).start()
            else:
                acc[head] = out
                total[head] = sums
                largest[head] = updated

    def forward(step, piece):
        incoming(step, piece).wait_recv()
        pl.when(step < depth)(lambda: send(step, step + 1, piece, above).start())
        start_pass(step, piece)

        @pl.when(step < depth)
        def _():
            incoming(REACH - step, piece).wait_recv()
            pl.when(step < depth - 1)(
                lambda: send(REACH - step, REACH - step - 1, piece, below).start()
            )
            start_pass(REACH - step, piece)

    def turn(head):
        q_turned[head] = q_scr.reshape(heads, tall, width)[head].T

    for k in range(kv_heads):
        q_local[k].wait()
    for k in range(kv_heads):
        pltpu.make_async_remote_copy(
            src_ref=q_scr.at[other * kv_heads + k],
            dst_ref=q_scr.at[other * kv_heads + k],
            send_sem=q_send_sem.at[k],
            recv_sem=q_sem.at[other, k],
            device_id=pair,
            device_id_type=MESH,
        ).wait_recv()

    def begin_piece(i, carry):
        piece = piece_at(i)
        forward(1, piece)
        for k in range(piece_heads):
            turn(piece * piece_heads + k)
        attend(0, piece, (), False)
        return carry

    lax.fori_loop(0, PIECES, begin_piece, 0)

    def middle(i, carry):
        step, piece = lax.div(i, PIECES) + 1, piece_at(lax.rem(i, PIECES))
        forward(step + 1, piece)
        both = [
            sum(equal(step, at) * backs[at][part] for at in range(1, depth)) for part in range(2)
        ]
        attend(step, piece, both, False)
        return carry

    lax.fori_loop(0, (depth - 1) * PIECES, middle, 0)

    def finish_piece(i, carry):
        attend(depth, piece_at(i), backs[depth], True)
        return carry

    lax.fori_loop(0, PIECES, finish_piece, 0)

    for i in range(own_pieces):
        to_pair(i).wait_send()
    for copy in q_remote:
        copy.wait_send()
    for slot in range(REACH):
        for piece in range(PIECES):
            if slot > 0:
                send(0, slot, piece, above).wait_send()
            lacking, copy = pass_on(slot, piece)
            pl.when(lacking)(copy.wait_send)
    for head in range(heads):
        write(head).wait()


def shards(queries, key_heads, value_head_rows, doc_lengths):
    kv_heads = key_heads.shape[1]
    rows = key_heads.shape[0] // 2
    width = key_heads.shape[2]
    group = queries.shape[1] // kv_heads
    heads = 2 * kv_heads
    tall = rows * group
    piece = (heads // PIECES, 2, rows, width)
    steps = REACH // 2 + 1
    any_space = pl.BlockSpec(memory_space=pl.ANY)
    return pl.pallas_call(
        functools.partial(kernel, lax.axis_size("ctx")),
        name="relay_attention",
        out_shape=jax.ShapeDtypeStruct((rows, heads * group, width), jnp.bfloat16),
        in_specs=[any_space] * 4,
        out_specs=any_space,
        scratch_shapes=[
            pltpu.VMEM((heads, rows, group, width), jnp.bfloat16),
            pltpu.VMEM((heads, width, tall), jnp.bfloat16),
            pltpu.VMEM((2 * REACH, PIECES, *piece), jnp.bfloat16),
            pltpu.VMEM((PIECES // 2, *piece), jnp.bfloat16),
            pltpu.VMEM((2, 2, rows, kv_heads, width), jnp.bfloat16),
            pltpu.VMEM((rows, kv_heads, width), jnp.float32),
            pltpu.VMEM((steps, 2 * rows, tall), jnp.float32),
            pltpu.VMEM((heads, width, tall), jnp.float32),
            pltpu.VMEM((heads, 1, tall), jnp.float32),
            pltpu.VMEM((heads, 1, tall), jnp.float32),
            pltpu.VMEM((heads, rows, group, width), jnp.bfloat16),
            pltpu.SMEM(doc_lengths.shape, jnp.int32),
            pltpu.SemaphoreType.DMA((2, 2)),
            pltpu.SemaphoreType.DMA,
            pltpu.SemaphoreType.DMA((2, kv_heads)),
            pltpu.SemaphoreType.DMA((kv_heads,)),
            pltpu.SemaphoreType.DMA((heads,)),
            pltpu.SemaphoreType.DMA((2 * REACH, PIECES)),
            pltpu.SemaphoreType.DMA((REACH, PIECES)),
            pltpu.SemaphoreType.DMA((REACH, PIECES)),
            pltpu.SemaphoreType.DMA((PIECES // 2,)),
        ],
        compiler_params=pltpu.CompilerParams(
            collective_id=0, has_side_effects=True, vmem_limit_bytes=61 << 20
        ),
    )(queries, key_heads, value_head_rows, doc_lengths)


def solution(mesh):
    in_specs = (P("ctx", "head", None), P("ctx", "head", None), P("ctx", "head", None), P())
    out_specs = P(("ctx", "head"), None, None)
    return jax.shard_map(shards, mesh=mesh, in_specs=in_specs, out_specs=out_specs, check_vma=False)
```

time: 52.5 us -> 39.4 us (0.75)
  Pallas kernels: 47.6 us -> 37 us
  local copies, waits for them, and re-layouts: 4.66 us -> 2.26 us
    pallas_call x1, Pallas kernels: 47.6 us -> 37 us  [shards(): pl.pallas_call(functools.partial(kernel, lax.axis_size('ctx')), name='rel...]
    unnamed x9 -> x1, local copies, waits for them, and re-layouts: 4.66 us -> 2.26 us
where the time goes in v1:
time: 39.4 us; the launch traced here: 39.3 us
  Pallas kernels  37 us (94%)
  local copies, waits for them, and re-layouts  2.26 us (6%)
    pallas_call x1, Pallas kernels, shards(): pl.pallas_call(functools.partial(kernel, lax.axis_size('ctx')), name='rel...  37 us
    unnamed x1, local copies, waits for them, and re-layouts  2.26 us

profile of v1, /device:TPU:24, one launch (start us, length us, event | category | flops | bytes accessed | tf_op | source)
XLA Modules:
  0.0 39.3 jit_solution(218052062949188692)
XLA Ops:
  0.0 37.0 %relay_attention.1 = bf16[64,64,128]{2,1,0:T(8,128)(2,1)} custom-call(bf16[128,32,128]{2,1,0:T(8,128)(2,1)} %q_hbm.1, bf16[128,4,128]{2,1,0:T(4,128)(2,1)} %k_hbm.1, bf16[128,4,128]{2,1,0:T(4,128)(2,1)} %v_hbm.1, s32[64]{0:T(128)} %len_hbm.1), custom_call_target="tpu_custom_call" | custom-call | tf_op jit(solution)/shard_map/relay_attention/pallas_call | solution.py:377
  37.0 2.3 %copy.6 = bf16[64,64,128]{2,1,0:T(8,128)(2,1)} copy(bf16[64,64,128]{2,1,0:T(8,128)(2,1)} %relay_attention.1) | data formatting | bytes 2097152

commit v2 on v1

--- a/solution.py
+++ b/solution.py
@@ -32,7 +32,7 @@
     k_hbm,
     v_hbm,
     len_hbm,
-    o_hbm,
+    o_ref,
     q_scr,
     q_turned,
     kv,
@@ -43,13 +43,11 @@
     acc,
     total,
     largest,
-    o_scr,
     lens,
     raw_sem,
     len_sem,
     q_sem,
     q_send_sem,
-    o_sem,
     recv_sem,
     send_sem,
     pass_sem,
@@ -250,13 +248,6 @@
 
     def slot_of(back):
         return back + (REACH - 1) * lax.div(back - spot + REACH - 1, REACH)
-
-    def write(head):
-        return pltpu.make_async_copy(
-            o_scr.at[head],
-            o_hbm.at[:, pl.ds(pl.multiple_of(head * group, group), group)],
-            o_sem.at[head],
-        )
 
     def attend(step, piece, backs, last):
         first = not backs
@@ -287,9 +278,8 @@
                 sums = total[head] * shrink + sums
                 out = acc[head] * shrink + out
             if last:
-                result = (out * (1.0 / sums)).T.astype(jnp.bfloat16)
-                o_scr.reshape(heads, tall, width)[head] = result
-                write(head).start()
+                result = (out * (1.0 / sums)).T.reshape(rows, group, width).astype(jnp.bfloat16)
+                o_ref[:, pl.ds(pl.multiple_of(head * group, group), group), :] = result
             else:
                 acc[head] = out
                 total[head] = sums
@@ -360,11 +350,13 @@
                 send(0, slot, piece, above).wait_send()
             lacking, copy = pass_on(slot, piece)
             pl.when(lacking)(copy.wait_send)
-    for head in range(heads):
-        write(head).wait()
 
 
 def shards(queries, key_heads, value_head_rows, doc_lengths):
+    queries, key_heads, value_head_rows, doc_lengths = (
+        pltpu.with_memory_space_constraint(a, pltpu.HBM)
+        for a in (queries, key_heads, value_head_rows, doc_lengths)
+    )
     kv_heads = key_heads.shape[1]
     rows = key_heads.shape[0] // 2
     width = key_heads.shape[2]
@@ -379,7 +371,7 @@
         name="relay_attention",
         out_shape=jax.ShapeDtypeStruct((rows, heads * group, width), jnp.bfloat16),
         in_specs=[any_space] * 4,
-        out_specs=any_space,
+        out_specs=pl.BlockSpec(memory_space=pltpu.VMEM),
         scratch_shapes=[
             pltpu.VMEM((heads, rows, group, width), jnp.bfloat16),
             pltpu.VMEM((heads, width, tall), jnp.bfloat16),
@@ -391,20 +383,18 @@
             pltpu.VMEM((heads, width, tall), jnp.float32),
             pltpu.VMEM((heads, 1, tall), jnp.float32),
             pltpu.VMEM((heads, 1, tall), jnp.float32),
-            pltpu.VMEM((heads, rows, group, width), jnp.bfloat16),
             pltpu.SMEM(doc_lengths.shape, jnp.int32),
             pltpu.SemaphoreType.DMA((2, 2)),
             pltpu.SemaphoreType.DMA,
             pltpu.SemaphoreType.DMA((2, kv_heads)),
             pltpu.SemaphoreType.DMA((kv_heads,)),
-            pltpu.SemaphoreType.DMA((heads,)),
             pltpu.SemaphoreType.DMA((2 * REACH, PIECES)),
             pltpu.SemaphoreType.DMA((REACH, PIECES)),
             pltpu.SemaphoreType.DMA((REACH, PIECES)),
             pltpu.SemaphoreType.DMA((PIECES // 2,)),
         ],
         compiler_params=pltpu.CompilerParams(
-            collective_id=0, has_side_effects=True, vmem_limit_bytes=61 << 20
+            collective_id=0, has_side_effects=True, vmem_limit_bytes=32 << 20
         ),
     )(queries, key_heads, value_head_rows, doc_lengths)
 

time: 39.4 us -> 37.5 us (0.952)
  local copies, waits for them, and re-layouts: 2.26 us -> 0.97 us
  Pallas kernels: 37 us -> 36.4 us
    unnamed x1, local copies, waits for them, and re-layouts: 2.26 us -> 0.97 us
    pallas_call x1, Pallas kernels: 37 us -> 36.4 us  [shards(): pl.pallas_call(functools.partial(kernel, lax.axis_size('ctx')), name='rel...]
where the time goes in v2:
time: 37.5 us; the launch traced here: 37.4 us
  Pallas kernels  36.4 us (97%)
  local copies, waits for them, and re-layouts  0.97 us (3%)
    pallas_call x1, Pallas kernels, shards(): pl.pallas_call(functools.partial(kernel, lax.axis_size('ctx')), name='rel...  36.4 us
    unnamed x1, local copies, waits for them, and re-layouts  0.97 us

profile of v2, /device:TPU:24, one launch (start us, length us, event | category | flops | bytes accessed | tf_op | source)
XLA Modules:
  0.0 37.4 jit_solution(8410299947307689440)
XLA Ops:
  0.0 36.4 %relay_attention.1 = bf16[64,64,128]{2,1,0:T(8,128)(2,1)S(1)} custom-call(bf16[128,32,128]{2,1,0:T(8,128)(2,1)} %q_hbm.1, bf16[128,4,128]{2,1,0:T(4,128)(2,1)} %k_hbm.1, bf16[128,4,128]{2,1,0:T(4,128)(2,1)} %v_hbm.1, s32[64]{0:T(128)} %len_hbm.1), custom_call_target="tpu_custom_call" | custom-call | tf_op jit(solution)/shard_map/relay_attention/pallas_call | solution.py:369
  36.4 1.0 %copy.6 = bf16[64,64,128]{2,1,0:T(8,128)(2,1)} copy(bf16[64,64,128]{2,1,0:T(8,128)(2,1)S(1)} %relay_attention.1) | data formatting | bytes 2097152

commit v3 on v2

--- a/solution.py
+++ b/solution.py
@@ -158,7 +158,7 @@
         return pltpu.make_async_remote_copy(
             src_ref=kv_out.at[i],
             dst_ref=kv.at[0, core * own_pieces + i],
-            send_sem=pair_sem.at[i],
+            send_sem=pair_sem,
             recv_sem=recv_sem.at[0, core * own_pieces + i],
             device_id=pair,
             device_id_type=MESH,
@@ -168,7 +168,7 @@
         return pltpu.make_async_remote_copy(
             src_ref=kv.at[slot, piece],
             dst_ref=kv.at[into, piece],
-            send_sem=send_sem.at[into, piece],
+            send_sem=send_sem.at[into],
             recv_sem=recv_sem.at[into, piece],
             device_id=target,
             device_id_type=MESH,
@@ -178,20 +178,23 @@
         return pltpu.make_async_remote_copy(
             src_ref=kv.at[slot, piece],
             dst_ref=kv.at[slot, piece],
-            send_sem=pair_sem.at[0],
+            send_sem=pair_sem,
             recv_sem=recv_sem.at[slot, piece],
             device_id=above,
             device_id_type=MESH,
         )
 
-    def pass_on(slot, piece):
+    def passing(slot):
         source = lax.rem(spot - slot + REACH, REACH)
         lacking = lax.div(source - spot_after + REACH, REACH)
-        into = 2 * REACH - 1 - lacking * (source - spot_after)
+        return lacking, 2 * REACH - 1 - lacking * (source - spot_after)
+
+    def pass_on(slot, piece):
+        lacking, into = passing(slot)
         copy = pltpu.make_async_remote_copy(
             src_ref=kv.at[slot, piece],
             dst_ref=kv.at[into, piece],
-            send_sem=pass_sem.at[slot, piece],
+            send_sem=pass_sem.at[slot],
             recv_sem=recv_sem.at[into, piece],
             device_id=after,
             device_id_type=MESH,
@@ -205,7 +208,6 @@
     def first_sends(piece):
         send(0, 1, piece, above).start()
         send(0, REACH - 1, piece, below).start()
-        start_pass(0, piece)
 
     def piece_at(i):
         half = lax.rem(core + lax.div(i, own_pieces), 2)
@@ -214,12 +216,18 @@
     for i in range(own_pieces):
         to_pair(i).start()
     for i in range(own_pieces):
-        first_sends(core * own_pieces + i)
+        pl.when(core == 0)(functools.partial(first_sends, i))
+        start_pass(0, core * own_pieces + i)
     for copy in q_remote:
         copy.start()
     for i in range(own_pieces):
-        incoming(0, other * own_pieces + i).wait_recv()
-        first_sends(other * own_pieces + i)
+        piece = other * own_pieces + i
+        incoming(0, piece).wait_recv()
+        pl.when(core == 1)(functools.partial(first_sends, own_pieces + i))
+        pl.when(core == 0)(functools.partial(first_sends, piece))
+        start_pass(0, piece)
+    for i in range(own_pieces):
+        pl.when(core == 1)(functools.partial(first_sends, i))
 
     len_copy.wait()
     place = node * rows + lax.broadcasted_iota(jnp.int32, (8, tall), 1) // group
@@ -334,22 +342,38 @@
 
     lax.fori_loop(0, (depth - 1) * PIECES, middle, 0)
 
+    def sent(block, sem):
+        pltpu.make_async_remote_copy(
+            src_ref=block,
+            dst_ref=block,
+            send_sem=sem,
+            recv_sem=recv_sem.at[0, 0],
+            device_id=pair,
+            device_id_type=MESH,
+        ).wait_send()
+
+    def sent_on(slot):
+        lacking, _ = passing(slot)
+        pl.when(lacking == 1)(functools.partial(sent, kv.at[slot], pass_sem.at[slot]))
+
+    sent(kv_out, pair_sem)
+    for copy in q_remote:
+        copy.wait_send()
+    for slot in (1, 2, 3, 6, 7):
+        sent(kv.at[slot], send_sem.at[slot])
+    for slot in (0, 1, 2, 6, 7):
+        sent_on(slot)
+
     def finish_piece(i, carry):
         attend(depth, piece_at(i), backs[depth], True)
         return carry
 
     lax.fori_loop(0, PIECES, finish_piece, 0)
 
-    for i in range(own_pieces):
-        to_pair(i).wait_send()
-    for copy in q_remote:
-        copy.wait_send()
-    for slot in range(REACH):
-        for piece in range(PIECES):
-            if slot > 0:
-                send(0, slot, piece, above).wait_send()
-            lacking, copy = pass_on(slot, piece)
-            pl.when(lacking)(copy.wait_send)
+    for slot in (4, 5):
+        sent(kv.at[slot], send_sem.at[slot])
+    for slot in (3, 4, 5):
+        sent_on(slot)
 
 
 def shards(queries, key_heads, value_head_rows, doc_lengths):
@@ -389,9 +413,9 @@
             pltpu.SemaphoreType.DMA((2, kv_heads)),
             pltpu.SemaphoreType.DMA((kv_heads,)),
             pltpu.SemaphoreType.DMA((2 * REACH, PIECES)),
-            pltpu.SemaphoreType.DMA((REACH, PIECES)),
-            pltpu.SemaphoreType.DMA((REACH, PIECES)),
-            pltpu.SemaphoreType.DMA((PIECES // 2,)),
+            pltpu.SemaphoreType.DMA((REACH,)),
+            pltpu.SemaphoreType.DMA((REACH,)),
+            pltpu.SemaphoreType.DMA,
         ],
         compiler_params=pltpu.CompilerParams(
             collective_id=0, has_side_effects=True, vmem_limit_bytes=32 << 20

time: 37.5 us -> 36.5 us (0.973)
  Pallas kernels: 36.4 us -> 35.4 us
    pallas_call x1, Pallas kernels: 36.4 us -> 35.4 us  [shards(): pl.pallas_call(functools.partial(kernel, lax.axis_size('ctx')), name='rel...]
where the time goes in v3:
time: 36.5 us; the launch traced here: 36.4 us
  Pallas kernels  35.4 us (97%)
  local copies, waits for them, and re-layouts  0.97 us (3%)
    pallas_call x1, Pallas kernels, shards(): pl.pallas_call(functools.partial(kernel, lax.axis_size('ctx')), name='rel...  35.4 us
    unnamed x1, local copies, waits for them, and re-layouts  0.97 us

profile of v3, /device:TPU:24, one launch (start us, length us, event | category | flops | bytes accessed | tf_op | source)
XLA Modules:
  0.0 36.4 jit_solution(16071864360431374633)
XLA Ops:
  0.0 35.4 %relay_attention.1 = bf16[64,64,128]{2,1,0:T(8,128)(2,1)S(1)} custom-call(bf16[128,32,128]{2,1,0:T(8,128)(2,1)} %q_hbm.1, bf16[128,4,128]{2,1,0:T(4,128)(2,1)} %k_hbm.1, bf16[128,4,128]{2,1,0:T(4,128)(2,1)} %v_hbm.1, s32[64]{0:T(128)} %len_hbm.1), custom_call_target="tpu_custom_call" | custom-call | tf_op jit(solution)/shard_map/relay_attention/pallas_call | solution.py:393
  35.4 1.0 %copy.6 = bf16[64,64,128]{2,1,0:T(8,128)(2,1)} copy(bf16[64,64,128]{2,1,0:T(8,128)(2,1)S(1)} %relay_attention.1) | data formatting | bytes 2097152

commit v4 on v3

--- a/solution.py
+++ b/solution.py
@@ -223,11 +223,10 @@
     for i in range(own_pieces):
         piece = other * own_pieces + i
         incoming(0, piece).wait_recv()
-        pl.when(core == 1)(functools.partial(first_sends, own_pieces + i))
         pl.when(core == 0)(functools.partial(first_sends, piece))
         start_pass(0, piece)
-    for i in range(own_pieces):
-        pl.when(core == 1)(functools.partial(first_sends, i))
+    for i in range(PIECES):
+        pl.when(core == 1)(functools.partial(first_sends, piece_at(i)))
 
     len_copy.wait()
     place = node * rows + lax.broadcasted_iota(jnp.int32, (8, tall), 1) // group

time: 36.5 us -> 36.2 us (level)
  no operation moved by 1% of the time
where the time goes in v4:
time: 36.2 us
  Pallas kernels  35.2 us (97%)
  local copies, waits for them, and re-layouts  0.97 us (3%)
    pallas_call x1, Pallas kernels, shards(): pl.pallas_call(functools.partial(kernel, lax.axis_size('ctx')), name='rel...  35.2 us
    unnamed x1, local copies, waits for them, and re-layouts  0.97 us

profile of v4, /device:TPU:24, one launch (start us, length us, event | category | flops | bytes accessed | tf_op | source)
XLA Modules:
  0.0 36.2 jit_solution(2770746239108277005)
XLA Ops:
  0.0 35.2 %relay_attention.1 = bf16[64,64,128]{2,1,0:T(8,128)(2,1)S(1)} custom-call(bf16[128,32,128]{2,1,0:T(8,128)(2,1)} %q_hbm.1, bf16[128,4,128]{2,1,0:T(4,128)(2,1)} %k_hbm.1, bf16[128,4,128]{2,1,0:T(4,128)(2,1)} %v_hbm.1, s32[64]{0:T(128)} %len_hbm.1), custom_call_target="tpu_custom_call" | custom-call | tf_op jit(solution)/shard_map/relay_attention/pallas_call | solution.py:392
  35.2 1.0 %copy.6 = bf16[64,64,128]{2,1,0:T(8,128)(2,1)} copy(bf16[64,64,128]{2,1,0:T(8,128)(2,1)S(1)} %relay_attention.1) | data formatting | bytes 2097152

commit v5 on v4

--- a/solution.py
+++ b/solution.py
@@ -52,6 +52,7 @@
     send_sem,
     pass_sem,
     pair_sem,
+    lead_sem,
 ):
     kv_heads = k_hbm.shape[1]
     heads = 2 * kv_heads
@@ -225,8 +226,16 @@
         incoming(0, piece).wait_recv()
         pl.when(core == 0)(functools.partial(first_sends, piece))
         start_pass(0, piece)
-    for i in range(PIECES):
-        pl.when(core == 1)(functools.partial(first_sends, piece_at(i)))
+    @pl.when(core == 0)
+    def _():
+        pl.semaphore_signal(lead_sem, inc=1, device_id=pair, device_id_type=MESH)
+
+    @pl.when(core == 1)
+    def _():
+        pl.semaphore_wait(lead_sem, 1)
+        for i in range(PIECES):
+            first_sends(piece_at(i))
+
 
     len_copy.wait()
     place = node * rows + lax.broadcasted_iota(jnp.int32, (8, tall), 1) // group
@@ -415,6 +424,7 @@
             pltpu.SemaphoreType.DMA((REACH,)),
             pltpu.SemaphoreType.DMA((REACH,)),
             pltpu.SemaphoreType.DMA,
+            pltpu.SemaphoreType.REGULAR,
         ],
         compiler_params=pltpu.CompilerParams(
             collective_id=0, has_side_effects=True, vmem_limit_bytes=32 << 20

time: 36.2 us -> 36.3 us (level)
  no operation moved by 1% of the time
where the time goes in v5:
time: 36.3 us; the launch traced here: 36.2 us
  Pallas kernels  35.2 us (97%)
  local copies, waits for them, and re-layouts  0.97 us (3%)
    pallas_call x1, Pallas kernels, shards(): pl.pallas_call(functools.partial(kernel, lax.axis_size('ctx')), name='rel...  35.2 us
    unnamed x1, local copies, waits for them, and re-layouts  0.97 us

profile of v5, /device:TPU:24, one launch (start us, length us, event | category | flops | bytes accessed | tf_op | source)
XLA Modules:
  0.0 36.2 jit_solution(4557108977104715534)
XLA Ops:
  0.0 35.2 %relay_attention.1 = bf16[64,64,128]{2,1,0:T(8,128)(2,1)S(1)} custom-call(bf16[128,32,128]{2,1,0:T(8,128)(2,1)} %q_hbm.1, bf16[128,4,128]{2,1,0:T(4,128)(2,1)} %k_hbm.1, bf16[128,4,128]{2,1,0:T(4,128)(2,1)} %v_hbm.1, s32[64]{0:T(128)} %len_hbm.1), custom_call_target="tpu_custom_call" | custom-call | tf_op jit(solution)/shard_map/relay_attention/pallas_call | solution.py:401
  35.2 1.0 %copy.6 = bf16[64,64,128]{2,1,0:T(8,128)(2,1)} copy(bf16[64,64,128]{2,1,0:T(8,128)(2,1)S(1)} %relay_attention.1) | data formatting | bytes 2097152
